TPU v7x, 512 devices: a whole 4x4x16 slice. The times are simulated.
512 devices in a mesh: section: 8 (over y, x_lo), expert: 64 (over x_hi, z, core).
Axes of the slice: x: 4 (x_hi: 2, x_lo: 2; x = x_hi * 2 + x_lo), y: 4, z: 16, core: 2. Of those that a mesh axis runs over, the one named last changes fastest.
Arguments:
- tokens: bfloat16 [8192, 3584], P('expert'), may hold values from -6 to 6
- norm_gain: bfloat16 [3584], replicated, may hold values from 0.25 to 1.75
- router: bfloat16 [3584, 64], replicated, may hold values from -0.09375 to 0.09375
- w_gate: bfloat16 [64, 3584, 1024], P('expert', None, 'section'), may hold values from -0.09375 to 0.09375
- w_up: bfloat16 [64, 3584, 1024], P('expert', None, 'section'), may hold values from -0.09375 to 0.09375
- w_down: bfloat16 [64, 1024, 3584], P('expert', 'section'), may hold values from -0.1875 to 0.1875
- expert_ids: int32 [8192, 3], P('expert'), may hold values from 0 to 63, all different within a row; in each aligned block of 128 rows (0 to 127, 128 to 255, ...) at most 9 rows name the same one
Outputs:
- layer_out: bfloat16 [8192, 3584], P('expert', 'section')
Inputs may be any that keep to these rules, and one draw needn't show every extreme that they name: `expert_ids`: each row names 3 different experts. Within each aligned block of 128 rows (the rows of one index of the expert axis) no expert is named by more than 9 rows, and in every draw some expert is named by exactly 9 rows of some block.
All inputs are finite; a program needn't handle non-finite values.
Results may differ from a plain program's by a relative error of at most 0.013.
Values may be sent and summed in bfloat16 or wider, within the bound.
A program may use at most 64 MiB of HBM per device.

v0:
```python
import jax
import jax.numpy as jnp
from jax import lax
from jax.sharding import PartitionSpec as P

EPSILON = 1e-06


def per_device(tokens, norm_gain, router, w_gate, w_up, w_down, expert_ids):
    tok_count, model_width = tokens.shape
    top_count = expert_ids.shape[1]
    expert_count = router.shape[1]
    cap_slots = tok_count * top_count * 3 // (2 * expert_count)
    pair_count = tok_count * top_count
    tokens_f = tokens.astype(jnp.float32)
    mean_sq = jnp.mean(tokens_f * tokens_f, axis=-1, keepdims=True)
    normed = (tokens_f * lax.rsqrt(mean_sq + EPSILON) * norm_gain.astype(jnp.float32)).astype(
        jnp.bfloat16
    )
    logits = jnp.dot(normed, router, preferred_element_type=jnp.float32)
    scores = jax.nn.sigmoid(logits)
    picked = jnp.take_along_axis(scores, expert_ids, axis=1)
    route_weight = 2.5 * picked / jnp.sum(picked, axis=1, keepdims=True)
    flat_ids = expert_ids.reshape(-1)
    onehot = (flat_ids[:, None] == jnp.arange(expert_count, dtype=jnp.int32)[None, :]).astype(
        jnp.float32
    )
    pair_rows = jnp.arange(pair_count, dtype=jnp.int32)
    earlier = (pair_rows[None, :] < pair_rows[:, None]).astype(jnp.float32)
    before = jnp.dot(
        earlier, onehot, precision=lax.Precision.HIGHEST, preferred_element_type=jnp.float32
    )
    slot_rank = jnp.sum(onehot * before, axis=1).astype(jnp.int32)
    slot_index = flat_ids * cap_slots + slot_rank
    copies = normed[pair_rows // top_count]
    buffer = (
        jnp.zeros((expert_count * cap_slots, model_width), jnp.bfloat16).at[slot_index].set(copies)
    )
    buffer = buffer.reshape(expert_count, cap_slots, model_width)
    received = lax.all_to_all(buffer, "expert", split_axis=0, concat_axis=0, tiled=True)
    gate_act = jnp.einsum("ecd,dh->ech", received, w_gate[0], preferred_element_type=jnp.float32)
    up_act = jnp.einsum("ecd,dh->ech", received, w_up[0], preferred_element_type=jnp.float32)
    hidden = (jax.nn.silu(gate_act) * up_act).astype(jnp.bfloat16)
    partial_value = jnp.einsum(
        "ech,hd->ecd", hidden, w_down[0], preferred_element_type=jnp.float32
    ).astype(jnp.bfloat16)
    returned = lax.all_to_all(partial_value, "expert", split_axis=0, concat_axis=0, tiled=True)
    ret_width = returned.shape[2]
    picked_rows = returned.reshape(expert_count * cap_slots, ret_width)[slot_index]
    picked_rows = picked_rows.reshape(tok_count, top_count, ret_width).astype(jnp.float32)
    mixed_sum = jnp.einsum("tkd,tk->td", picked_rows, route_weight)
    shares = lax.psum_scatter(
        mixed_sum.astype(jnp.bfloat16), "section", scatter_dimension=1, tiled=True
    ).astype(jnp.float32)
    out_width = shares.shape[1]
    residual = lax.dynamic_slice_in_dim(tokens, lax.axis_index("section") * out_width, out_width, 1)
    return (residual.astype(jnp.float32) + shares).astype(jnp.bfloat16)


def solution(mesh):
    placed = (
        P("expert", None),
        P(),
        P(),
        P("expert", None, "section"),
        P("expert", None, "section"),
        P("expert", "section", None),
        P("expert", None),
    )
    return jax.shard_map(
        per_device, mesh=mesh, in_specs=placed, out_specs=P("expert", "section"), check_vma=False
    )
```

profile of v0, /device:TPU:4, one launch (start us, length us, event | category | flops | bytes accessed | tf_op | source)
XLA Modules:
  0.0 827.2 jit_solution(5354434116945198552)
XLA Ops:
  6.6 0.8 broadcast_multiply_fusion
  7.3 0.8 copy.32
  8.1 1.4 fusion.7
  9.6 0.7 convert_element_type.47
  11.1 1.5 fusion.9
  12.5 15.3 %scatter_custom_fusion = bf16[576,3584]{1,0:T(8,128)(2,1)} fusion(s32[384]{0:T(512)S(1)} %fusion.33, bf16[128,3584]{1,0:T(8,128)(2,1)S(1)} %fusion.9, s32[1024]{0:T(1024)S(1)} %pad_clamp_fusion.1, bf16[]{:T(256)} %constant.18.clone.1), kind=kCustom, calls=%fused_computation.6 | custom fusion | bytes 4128770 | tf_op jit(solution)/shard_map/scatter | solution.py:37
  27.9 7.7 reshape.105
  35.5 340.5 %all_to_all.10 = bf16[64,9,3584]{2,1,0:T(8,128)(2,1)S(1)} all-to-all(bf16[64,9,3584]{2,1,0:T(8,128)(2,1)} %reshape.105), channel_id=1, replica_groups=mesh['section'=8,'expert'=64] {'expert'}, dimensions={0} | all-to-all | bytes 8257536 | tf_op jit(solution)/shard_map/all_to_all | solution.py:40
  376.1 3.0 copy-done.1
  379.1 4.4 fusion.5
  383.5 9.7 %convolution_convert_fusion = bf16[64,9,3584]{2,0,1:T(8,128)(2,1)} fusion(bf16[64,9,3584]{2,1,0:T(8,128)(2,1)} %copy-done.1, bf16[1,128,3584]{2,1,0:T(8,128)(2,1)S(1)} %copy-done, bf16[1,3584,128]{2,1,0:T(8,128)(2,1)S(1)} %copy-done.2, f32[64,9,128]{2,0,1:T(8,128)S(1)} %fusion.5), kind=kOutput, calls=%fused_computation.5 | convolution fusion | flops 1059471360 | bytes 10387456 | tf_op jit(solution)/shard_map/ech,hd->ecd/dot_general | solution.py:44
  393.3 7.8 copy.35
  401.0 18.6 %all-to-all-start.1 = ((bf16[64,9,3584]{2,1,0:T(8,128)(2,1)}), bf16[64,9,3584]{2,1,0:T(8,128)(2,1)}, u32[]{:S(2)}, u32[]{:S(2)}) async-start(bf16[64,9,3584]{2,1,0:T(8,128)(2,1)} %copy.35), calls=%async_computation.1 | async-start | bytes 14680064 | tf_op jit(solution)/shard_map/all_to_all | solution.py:47
  420.0 0.4 fusion.21
  420.5 2.9 gather_fusion.1
  423.8 318.7 %all-to-all-done.1 = bf16[64,9,3584]{2,1,0:T(8,128)(2,1)} async-done(((bf16[64,9,3584]{2,1,0:T(8,128)(2,1)}), bf16[64,9,3584]{2,1,0:T(8,128)(2,1)}, u32[]{:S(2)}, u32[]{:S(2)}) %all-to-all-start.1) | async-done | bytes 4128800 | tf_op jit(solution)/shard_map/all_to_all | solution.py:47
  742.5 8.0 reshape.106
  750.5 10.3 %gather_fusion = bf16[384,3584]{1,0:T(8,128)(2,1)} fusion(bf16[576,3584]{1,0:T(8,128)(2,1)} %reshape.106, s32[1024]{0:T(1024)S(1)} %pad_clamp_fusion), kind=kCustom, calls=%fused_computation.1 | custom fusion | bytes 5506560 | tf_op jit(solution)/shard_map/gather | solution.py:49
  760.8 6.7 reshape.107
  767.4 7.3 multiply_reduce_fusion
  774.8 1.3 copy.41
  776.1 1.0 constant_dynamic-slice_fusion
  777.3 41.4 %reduce-scatter.2.cloned.1.call-done = bf16[128,448]{0,1:T(8,128)(2,1)} async-done(((bf16[128,3584]{0,1:T(8,128)(2,1)}), bf16[128,448]{0,1:T(8,128)(2,1)}) %reduce-scatter.2.cloned.1.call-update) | async-done | bytes 114704 | tf_op jit(solution)/shard_map/reduce_scatter | solution.py:52
  818.6 1.6 add_convert_fusion
  (32 shorter events, 1.8 us)
Async XLA Ops:
  6.5 377.0 %copy-start = (bf16[1,128,3584]{2,1,0:T(8,128)(2,1)S(1)}, bf16[1,128,3584]{2,1,0:T(8,128)(2,1)}, u32[]{:S(2)}) copy-start(bf16[1,128,3584]{2,1,0:T(8,128)(2,1)} %param.12) | copy-start | bytes 2752516
  35.5 343.6 %copy-start.5 = (bf16[1,3584,128]{2,1,0:T(8,128)(2,1)S(1)}, bf16[1,3584,128]{2,1,0:T(8,128)(2,1)}, u32[]{:S(2)}) copy-start(bf16[1,3584,128]{2,1,0:T(8,128)(2,1)} %param.10) | copy-start | bytes 2752516
  376.1 3.0 copy-start.1
  379.1 4.4 copy-start.2
  401.0 18.6 %copy-start.4 = (s32[128,3]{0,1:T(4,128)S(1)}, s32[128,3]{0,1:T(4,128)}, u32[]{:S(2)}) copy-start(s32[128,3]{0,1:T(4,128)} %param.13) | copy-start | bytes 4612
  401.0 19.0 %copy-start.3 = (bf16[3584,64]{0,1:T(8,128)(2,1)S(1)}, bf16[3584,64]{0,1:T(8,128)(2,1)}, u32[]{:S(2)}) copy-start(bf16[3584,64]{0,1:T(8,128)(2,1)} %param.9) | copy-start | bytes 1376260
  401.0 341.4 %all-to-all-start.1 = ((bf16[64,9,3584]{2,1,0:T(8,128)(2,1)}), bf16[64,9,3584]{2,1,0:T(8,128)(2,1)}, u32[]{:S(2)}, u32[]{:S(2)}) async-start(bf16[64,9,3584]{2,1,0:T(8,128)(2,1)} %copy.35), calls=%async_computation.1 | async-start | bytes 14680064 | tf_op jit(solution)/shard_map/all_to_all | solution.py:47
  419.6 399.0 %reduce-scatter.2.cloned.1.call-start = ((), (), s32[]{:S(2)}) async-start(), calls=%async_computation.3 | async-start | bytes 1032192 | tf_op jit(solution)/shard_map/reduce_scatter | solution.py:52
Sparse Core Ops, SparseCore 0:
  776.2 42.3 reduce-scatter.1
where the time goes:
time: 838 us; the launch traced here: 827 us
  waiting for transfers between devices  360 us (43%)
  blocking collectives  341 us (41%)
  local copies, waits for them, and re-layouts  66.1 us (8%)
  starting transfers between devices  18.6 us (2%)
  matrix products  14.8 us (2%)
  between operations  13.7 us (2%)
  other arithmetic  13.4 us (2%)
    all_to_all x1, blocking collectives, per_device(): lax.all_to_all(buffer, 'expert', split_axis=0, concat_axis=0, tiled=True)  341 us
    all_to_all x1, waiting for transfers between devices, per_device(): lax.all_to_all(partial_value, 'expert', split_axis=0, concat_axis=0, tile...  319 us
    reduce_scatter x1, waiting for transfers between devices, per_device(): lax.psum_scatter(mixed_sum.astype(jnp.bfloat16), 'section', scatter_dimen...  41.4 us
    all_to_all x1, starting transfers between devices, per_device(): lax.all_to_all(partial_value, 'expert', split_axis=0, concat_axis=0, tile...  18.6 us
  transfers between devices with their start and end apart: 2, of which 2 were waited for; matrix products, arithmetic and copies ran while one was open for 1% of the time, Pallas kernels for 0%

commit v1 on v0

v1 whole, which is shorter than its diff:
```python
import functools

import jax
import jax.numpy as jnp
from jax import lax
from jax.experimental import pallas as pl
from jax.experimental.pallas import tpu as pltpu
from jax.sharding import PartitionSpec as P

EPSILON = 1e-06
MESH = pl.DeviceIdType.MESH
F32 = jnp.float32
BF16 = jnp.bfloat16
LANES = 128
MAIN = 8
Y = 4
CHUNKS = 4


def iota(shape, dim):
    return lax.broadcasted_iota(jnp.int32, shape, dim)


def onehot(mask):
    return jnp.where(mask, 1.0, 0.0).astype(BF16)


def dot(a, b):
    return jnp.dot(a, b, preferred_element_type=F32)


def dot_t(a, b):
    return lax.dot_general(a, b, (((0,), (0,)), ((), ())), preferred_element_type=F32)


def lane_tiles(rows, count, step):
    return jnp.concatenate([rows[j * step : (j + 1) * step] for j in range(count)], axis=1)


def row_tiles(cols, count):
    return jnp.concatenate([cols[:, j * LANES : (j + 1) * LANES] for j in range(count)], axis=0)


def kernel(
    z_size,
    ids_ref,
    tok_ref,
    gain_ref,
    router_ref,
    wg_hbm,
    wu_hbm,
    wd_hbm,
    out_ref,
    dsend,
    xin,
    wgu,
    wdn,
    gown,
    gsend,
    grecv,
    hbuf,
    keep,
    xsend,
    xrecv,
    rsend,
    rrecv,
    csend,
    crecv,
    d_s,
    d_r,
    l_s,
    l_r,
    w_s,
    w_r,
    g_s,
    g_r,
    h_s,
    h_r,
    x_s,
    x_r,
    r_s,
    r_r,
    c_s,
    c_r,
):
    section = lax.axis_index("section")
    expert = lax.axis_index("expert")
    y, x_lo = section // 2, section % 2
    core = expert % 2
    z = (expert // 2) % z_size
    x_hi = expert // (2 * z_size)
    other_core = (core + x_lo) % 2
    peers = dsend.shape[0]
    per_chunk = peers // CHUNKS
    tok_count, width = tok_ref.shape
    part_width = width // Y
    tiles = part_width // LANES
    experts = router_ref.shape[1]

    def peer_expert(i, sign=1):
        half = (i // 2 + 1) // 2
        shift = half * (2 * ((i // 2) % 2) - 1)
        hi = (x_hi + i % 2) % 2
        return (hi * z_size + (z + sign * shift + 2 * z_size) % z_size) * 2 + other_core

    def y_peer(r):
        return ((y + r) % Y) * 2 + x_lo

    x_peer = y * 2 + 1 - x_lo

    def to(section_to, expert_to):
        return {"section": section_to, "expert": expert_to}

    barrier = pltpu.get_barrier_semaphore()

    def greet(i, carry):
        pl.semaphore_signal(
            barrier, inc=1, device_id=to(section, peer_expert(i)), device_id_type=MESH
        )
        return carry

    for r in range(1, Y):
        pl.semaphore_signal(barrier, inc=1, device_id=to(y_peer(r), expert), device_id_type=MESH)
    pl.semaphore_signal(barrier, inc=1, device_id=to(x_peer, expert), device_id_type=MESH)

    @pl.when(x_lo == 1)
    def _():
        greet(0, 0)

    lax.fori_loop(1, peers, greet, 0)

    def rows_of(r):
        return pl.ds(pl.multiple_of(((y + r) % Y) * part_width, LANES), part_width)

    own_weights = [
        pltpu.make_async_copy(wg_hbm.at[0, rows_of(0), :], wgu.at[0, :, 0:LANES], w_r.at[0, 0]),
        pltpu.make_async_copy(
            wu_hbm.at[0, rows_of(0), :], wgu.at[0, :, LANES : 2 * LANES], w_r.at[1, 0]
        ),
        pltpu.make_async_copy(wd_hbm.at[0, :, rows_of(0)], wdn.at[0], w_r.at[2, 0]),
    ]
    for copy in own_weights:
        copy.start()

    square_sum = jnp.zeros((tok_count, LANES), F32)
    for j in range(width // LANES):
        piece = tok_ref[:, j * LANES : (j + 1) * LANES].astype(F32)
        square_sum = square_sum + piece * piece
    mean_sq = jnp.sum(square_sum, axis=1, keepdims=True) / width
    scale = lax.rsqrt(mean_sq + EPSILON)

    columns = pl.ds(pl.multiple_of(y * part_width, LANES), part_width)
    mine = (
        tok_ref[:, columns].astype(F32) * scale * gain_ref[:, columns].astype(F32)
    ).astype(BF16)

    ids = ids_ref[...]
    top = ids.shape[1]
    names = [ids[:, k : k + 1] for k in range(top)]
    expert_lane = iota((tok_count, experts), 1)
    picks = [jnp.where(name == expert_lane, 1.0, 0.0) for name in names]
    chosen = functools.reduce(jnp.add, picks)
    earlier = onehot(iota((tok_count, tok_count), 1) < iota((tok_count, tok_count), 0))
    before = dot(earlier, chosen.astype(BF16))
    slots = [jnp.sum(pick * before, axis=1, keepdims=True).astype(jnp.int32) for pick in picks]

    rows = peers * MAIN
    row_lane = iota((tok_count, rows), 1)
    row_name = peer_expert(row_lane // MAIN)
    row_slot = row_lane % MAIN
    main_of = [onehot((n == row_name) & (s == row_slot)) for n, s in zip(names, slots)]
    main = dot_t(functools.reduce(jnp.add, main_of), mine)
    last_of = [jnp.where((n == row_name) & (s == MAIN), 1.0, 0.0) for n, s in zip(names, slots)]
    last_any = functools.reduce(jnp.add, last_of)
    last = jnp.zeros((rows, LANES), F32)
    for j in range(tiles):
        pick_row = jnp.where(row_slot == j, last_any, 0.0).astype(BF16)
        last = last + dot_t(pick_row, mine[:, j * LANES : (j + 1) * LANES])
    dsend[...] = (
        jnp.concatenate([main, last], axis=1)
        .astype(BF16)
        .reshape(peers, MAIN, part_width + LANES)
    )

    pl.semaphore_wait(barrier, peers - 1 + x_lo + Y)

    def dispatch(i):
        return pltpu.make_async_remote_copy(
            src_ref=dsend.at[i],
            dst_ref=xin.at[0, i],
            send_sem=d_s.at[i],
            recv_sem=d_r.at[i],
            device_id=to(section, peer_expert(i)),
            device_id_type=MESH,
        )

    own_rows = pltpu.make_async_copy(dsend.at[0], xin.at[0, 0], d_r.at[0])

    @pl.when(x_lo == 0)
    def _():
        own_rows.start()

    @pl.when(x_lo == 1)
    def _():
        dispatch(0).start()

    def start_dispatch(i, carry):
        dispatch(i).start()
        return carry

    lax.fori_loop(1, peers, start_dispatch, 0)

    def weight_copies(r):
        there = to(y_peer(r), expert)
        lands = Y - r
        return [
            pltpu.make_async_remote_copy(
                wg_hbm.at[0, rows_of(r), :],
                wgu.at[lands, :, 0:LANES],
                w_s.at[0, r],
                w_r.at[0, lands],
                device_id=there,
                device_id_type=MESH,
            ),
            pltpu.make_async_remote_copy(
                wu_hbm.at[0, rows_of(r), :],
                wgu.at[lands, :, LANES : 2 * LANES],
                w_s.at[1, r],
                w_r.at[1, lands],
                device_id=there,
                device_id_type=MESH,
            ),
            pltpu.make_async_remote_copy(
                wd_hbm.at[0, :, rows_of(r)],
                wdn.at[lands],
                w_s.at[2, r],
                w_r.at[2, lands],
                device_id=there,
                device_id_type=MESH,
            ),
        ]

    weights = {r: weight_copies(r) for r in range(1, Y)}
    for which in range(3):
        for r in (2, 1, 3):
            weights[r][which].start()

    logits = jnp.zeros((tok_count, experts), F32)
    step = width // 7
    for j in range(7):
        cut = slice(j * step, (j + 1) * step)
        normed = (tok_ref[:, cut].astype(F32) * scale * gain_ref[:, cut].astype(F32)).astype(BF16)
        logits = logits + dot(normed, router_ref[cut, :])
    scores = jax.nn.sigmoid(logits)
    picked = [jnp.sum(pick * scores, axis=1, keepdims=True) for pick in picks]
    picked_sum = functools.reduce(jnp.add, picked)
    route = [2.5 * p / picked_sum for p in picked]

    def chunk(q):
        return pl.ds(q * per_chunk, per_chunk)

    def relay(q):
        return pltpu.make_async_remote_copy(
            src_ref=xin.at[0, chunk(q)],
            dst_ref=xin.at[1, chunk(q)],
            send_sem=l_s.at[q],
            recv_sem=l_r.at[q],
            device_id=to(x_peer, expert),
            device_id_type=MESH,
        )

    def wait_dispatch(i, carry):
        dispatch(i).wait_recv()
        return carry

    def stage_relay(q):
        lax.fori_loop(q * per_chunk, (q + 1) * per_chunk, wait_dispatch, 0)
        relay(q).start()

    def gate_copy(q, r):
        return pltpu.make_async_remote_copy(
            src_ref=gsend.at[q, r],
            dst_ref=grecv.at[q, Y - r],
            send_sem=g_s.at[q, r],
            recv_sem=g_r.at[q, Y - r],
            device_id=to(y_peer(r), expert),
            device_id_type=MESH,
        )

    def gate_arrival(q, r):
        return pltpu.make_async_remote_copy(
            src_ref=gsend.at[q, r],
            dst_ref=grecv.at[q, r],
            send_sem=g_s.at[q, r],
            recv_sem=g_r.at[q, r],
            device_id=to(y_peer(r), expert),
            device_id_type=MESH,
        )

    def hidden_copy(q, r):
        return pltpu.make_async_remote_copy(
            src_ref=hbuf.at[q, 0],
            dst_ref=hbuf.at[q, Y - r],
            send_sem=h_s.at[q, r],
            recv_sem=h_r.at[q, Y - r],
            device_id=to(y_peer(r), expert),
            device_id_type=MESH,
        )

    def hidden_arrival(q, r):
        return pltpu.make_async_remote_copy(
            src_ref=hbuf.at[q, 0],
            dst_ref=hbuf.at[q, r],
            send_sem=h_s.at[q, r],
            recv_sem=h_r.at[q, r],
            device_id=to(y_peer(r), expert),
            device_id_type=MESH,
        )

    def pair_copy(q):
        return pltpu.make_async_remote_copy(
            src_ref=xsend.at[q],
            dst_ref=xrecv.at[q],
            send_sem=x_s.at[q],
            recv_sem=x_r.at[q],
            device_id=to(x_peer, expert),
            device_id_type=MESH,
        )

    def returns(i):
        return pltpu.make_async_remote_copy(
            src_ref=rsend.at[i],
            dst_ref=rrecv.at[i],
            send_sem=r_s.at[i],
            recv_sem=r_r.at[i],
            device_id=to(section, peer_expert(i, -1)),
            device_id_type=MESH,
        )

    half_rows = per_chunk * MAIN
    lasts = 2 * per_chunk

    def stage_gate(q):
        relay(q).wait_recv()
        both = jnp.concatenate(
            [
                xin[c, q * per_chunk : (q + 1) * per_chunk].reshape(half_rows, part_width + LANES)
                for c in range(2)
            ],
            axis=0,
        )
        tail = both[:, part_width:]
        at = iota((tiles * lasts, 2 * half_rows), 0)
        pick = onehot(iota((tiles * lasts, 2 * half_rows), 1) == (at % lasts) * MAIN + at // lasts)
        last_rows = lane_tiles(dot(pick, tail), tiles, lasts).astype(BF16)
        inputs = jnp.concatenate([both[:, :part_width], last_rows], axis=0)
        for r in (2, 1, 3):
            gsend[q, r] = dot(inputs, wgu[r]).astype(BF16)
            gate_copy(q, r).start()
        gown[q] = dot(inputs, wgu[0])

    def stage_hidden(q):
        total = gown[q]
        for r in (1, 3, 2):
            gate_arrival(q, r).wait_recv()
            total = total + grecv[q, r].astype(F32)
        gate, up = total[:, :LANES], total[:, LANES:]
        hbuf[q, 0] = (gate / (1.0 + jnp.exp(-gate)) * up).astype(BF16)
        for r in (2, 1, 3):
            hidden_copy(q, r).start()

    def stage_down(q):
        for r in range(1, Y):
            hidden_arrival(q, r).wait_recv()
        hidden = jnp.concatenate([hbuf[q, r] for r in range(Y)], axis=1)
        down = jnp.concatenate([wdn[r] for r in range(Y)], axis=0)
        result = dot(hidden, down)
        last_rows = row_tiles(result[2 * half_rows :], tiles).astype(BF16)
        to_row = iota((2 * half_rows, tiles * lasts), 0)
        at = iota((2 * half_rows, tiles * lasts), 1)
        tail = dot(onehot((at % lasts) * MAIN + at // lasts == to_row), last_rows)
        message = jnp.concatenate([result[: 2 * half_rows], tail], axis=1)
        xsend[q] = message[half_rows:].astype(BF16)
        pair_copy(q).start()
        keep[q] = message[:half_rows]

    def start_return(i, carry):
        returns(i).start()
        return carry

    own_return = pltpu.make_async_copy(rsend.at[0], rrecv.at[0], r_r.at[0])

    def stage_return(q):
        pair_copy(q).wait_recv()
        full = keep[q] + xrecv[q].astype(F32)
        rsend[q * per_chunk : (q + 1) * per_chunk] = full.astype(BF16).reshape(
            per_chunk, MAIN, part_width + LANES
        )
        first = q * per_chunk
        if q == 0:

            @pl.when(x_lo == 0)
            def _():
                own_return.start()

            @pl.when(x_lo == 1)
            def _():
                returns(0).start()

            first = 1
        lax.fori_loop(first, (q + 1) * per_chunk, start_return, 0)

    def wait_weights(kinds):
        for which in kinds:
            own_weights[which].wait()
            for r in (1, 3, 2):
                weights[Y - r][which].wait_recv()

    stages = [stage_relay, stage_gate, stage_hidden, stage_down, stage_return]
    for step_at in range(CHUNKS + len(stages) - 1):
        for number in range(len(stages)):
            q = step_at - number
            if 0 <= q < CHUNKS:
                if number == 1 and q == 0:
                    wait_weights((0, 1))
                if number == 3 and q == 0:
                    wait_weights((2,))
                stages[number](q)

    def wait_return(i, carry):
        returns(i).wait_recv()
        return carry

    lax.fori_loop(0, peers, wait_return, 0)
    back = rrecv[...].reshape(rows, part_width + LANES)
    at = iota((tiles * peers, rows), 0)
    pick = onehot(iota((tiles * peers, rows), 1) == (at % peers) * MAIN + at // peers)
    last_rows = lane_tiles(dot(pick, back[:, part_width:]), tiles, peers).astype(BF16)
    table = jnp.concatenate([back[:, :part_width], last_rows], axis=0)
    peer_name = peer_expert(iota((tok_count, peers), 1))
    mixed = jnp.zeros((tok_count, part_width), F32)
    for k in range(top):
        ninth = onehot((names[k] == peer_name) & (slots[k] == MAIN))
        select = jnp.concatenate([main_of[k], ninth], axis=1)
        mixed = mixed + route[k] * dot(select, table)

    out_width = out_ref.shape[1]
    window = csend.shape[1]
    start_hi = part_width - window

    @pl.when(x_lo == 0)
    def _():
        csend[...] = mixed[:, start_hi:].astype(BF16)

    @pl.when(x_lo == 1)
    def _():
        csend[...] = mixed[:, :window].astype(BF16)

    swap = pltpu.make_async_remote_copy(
        csend, crecv, c_s, c_r, device_id=to(x_peer, expert), device_id_type=MESH
    )
    swap.start()
    swap.wait_recv()

    @pl.when(x_lo == 0)
    def _():
        residual = tok_ref[:, pl.ds(pl.multiple_of(y * part_width, LANES), window)].astype(F32)
        total = residual + (mixed[:, :window] + crecv[...].astype(F32))
        out_ref[...] = total[:, :out_width].astype(BF16)

    @pl.when(x_lo == 1)
    def _():
        residual = tok_ref[
            :, pl.ds(pl.multiple_of(y * part_width + start_hi, LANES), window)
        ].astype(F32)
        total = residual + (mixed[:, start_hi:] + crecv[...].astype(F32))
        out_ref[...] = total[:, window - out_width :].astype(BF16)

    swap.wait_send()

    def wait_sends(i, carry):
        dispatch(i).wait_send()
        returns(i).wait_send()
        return carry

    @pl.when(x_lo == 1)
    def _():
        wait_sends(0, 0)

    lax.fori_loop(1, peers, wait_sends, 0)
    for r in range(1, Y):
        for copy in weights[r]:
            copy.wait_send()
    for q in range(CHUNKS):
        relay(q).wait_send()
        pair_copy(q).wait_send()
        for r in range(1, Y):
            gate_copy(q, r).wait_send()
            hidden_copy(q, r).wait_send()


def per_device(z_size, n_section, tokens, norm_gain, router, w_gate, w_up, w_down, expert_ids):
    tok_count, width = tokens.shape
    part_width = width // Y
    message = part_width + LANES
    peers = 2 * z_size
    per_chunk = peers // CHUNKS
    chunk_rows = 2 * per_chunk * (MAIN + 1)
    half_rows = per_chunk * MAIN
    out_width = width // n_section
    window = -(-out_width // LANES) * LANES
    vmem = pl.BlockSpec(memory_space=pltpu.VMEM)
    hbm = pl.BlockSpec(memory_space=pl.ANY)
    dma = pltpu.SemaphoreType.DMA
    return pl.pallas_call(
        functools.partial(kernel, z_size),
        out_shape=jax.ShapeDtypeStruct((tok_count, out_width), BF16),
        in_specs=[vmem] * 4 + [hbm] * 3,
        out_specs=vmem,
        scratch_shapes=[
            pltpu.VMEM((peers, MAIN, message), BF16),
            pltpu.VMEM((2, peers, MAIN, message), BF16),
            pltpu.VMEM((Y, part_width, 2 * LANES), BF16),
            pltpu.VMEM((Y, LANES, part_width), BF16),
            pltpu.VMEM((CHUNKS, chunk_rows, 2 * LANES), F32),
            pltpu.VMEM((CHUNKS, Y, chunk_rows, 2 * LANES), BF16),
            pltpu.VMEM((CHUNKS, Y, chunk_rows, 2 * LANES), BF16),
            pltpu.VMEM((CHUNKS, Y, chunk_rows, LANES), BF16),
            pltpu.VMEM((CHUNKS, half_rows, message), F32),
            pltpu.VMEM((CHUNKS, half_rows, message), BF16),
            pltpu.VMEM((CHUNKS, half_rows, message), BF16),
            pltpu.VMEM((peers, MAIN, message), BF16),
            pltpu.VMEM((peers, MAIN, message), BF16),
            pltpu.VMEM((tok_count, window), BF16),
            pltpu.VMEM((tok_count, window), BF16),
            dma((peers,)),
            dma((peers,)),
            dma((CHUNKS,)),
            dma((CHUNKS,)),
            dma((3, Y)),
            dma((3, Y)),
            dma((CHUNKS, Y)),
            dma((CHUNKS, Y)),
            dma((CHUNKS, Y)),
            dma((CHUNKS, Y)),
            dma((CHUNKS,)),
            dma((CHUNKS,)),
            dma((peers,)),
            dma((peers,)),
            dma,
            dma,
        ],
        compiler_params=pltpu.CompilerParams(collective_id=0, has_side_effects=True),
    )(expert_ids, tokens, norm_gain.reshape(1, width), router, w_gate, w_up, w_down)


def solution(mesh):
    n_section, n_expert = mesh.shape["section"], mesh.shape["expert"]
    placed = (
        P("expert", None),
        P(),
        P(),
        P("expert", None, "section"),
        P("expert", None, "section"),
        P("expert", "section", None),
        P("expert", None),
    )
    return jax.shard_map(
        functools.partial(per_device, n_expert // 4, n_section),
        mesh=mesh,
        in_specs=placed,
        out_specs=P("expert", "section"),
        check_vma=False,
    )
```

time: 838 us -> 112 us (0.13); the launches traced: 827 us -> 112 us
  waiting for transfers between devices: 360 us -> 0 us
  blocking collectives: 341 us -> 0 us
  Pallas kernels: 0 us -> 106 us
  local copies, waits for them, and re-layouts: 66.1 us -> 5.99 us
  starting transfers between devices: 18.6 us -> 0 us
  matrix products: 14.8 us -> 0 us
  between operations: 13.7 us -> 0.01 us
  other arithmetic: 13.4 us -> 0 us
    all_to_all x1 -> x0, blocking collectives: 341 us -> none  [per_device(): lax.all_to_all(buffer, 'expert', split_axis=0, concat_axis=0, tiled=True)]
    all_to_all x1 -> x0, waiting for transfers between devices: 319 us -> none  [per_device(): lax.all_to_all(partial_value, 'expert', split_axis=0, concat_axis=0, tile...]
    pallas_call x0 -> x1, Pallas kernels: none -> 106 us  [per_device(): pl.pallas_call(functools.partial(kernel, z_size), out_shape=jax.ShapeDtyp...]
    reduce_scatter x1 -> x0, waiting for transfers between devices: 41.4 us -> none  [per_device(): lax.psum_scatter(mixed_sum.astype(jnp.bfloat16), 'section', scatter_dimen...]
    reshape x3 -> x1, local copies, waits for them, and re-layouts: 22.3 us -> 1.31 us  [per_device(): norm_gain.reshape(1, width)]
    all_to_all x1 -> x0, starting transfers between devices: 18.6 us -> none  [per_device(): lax.all_to_all(partial_value, 'expert', split_axis=0, concat_axis=0, tile...]
    scatter x1 -> x0, local copies, waits for them, and re-layouts: 15.3 us -> none  [per_device(): jnp.zeros((expert_count * cap_slots, model_width), jnp.bfloat16)]
    dot_general x4 -> x0, matrix products: 14.8 us -> none  [the longest x1 9.72 us: per_device(): jnp.einsum('ech,hd->ecd', hidden, w_down[0], preferred_element_type=jnp.f...]
  transfers between devices with their start and end apart: 2 -> 0, of which waited for: 2 -> 0; matrix products, arithmetic and copies ran while one was open for 1% -> 0% of each run, Pallas kernels for 0% -> 0%
where the time goes in v1:
time: 112 us
  Pallas kernels  106 us (95%)
  local copies, waits for them, and re-layouts  5.99 us (5%)
    pallas_call x1, Pallas kernels, per_device(): pl.pallas_call(functools.partial(kernel, z_size), out_shape=jax.ShapeDtyp...  106 us
    unnamed x4, local copies, waits for them, and re-layouts  3.01 us

profile of v1, /device:TPU:4, one launch (start us, length us, event | category | flops | bytes accessed | tf_op | source)
XLA Modules:
  0.0 111.5 jit_solution(7997122685541378596)
XLA Ops:
  0.0 0.0 copy-start
  0.0 1.3 %reshape.3.gain_ref = bf16[1,3584]{1,0:T(2,128)(2,1)} reshape(bf16[3584]{0:T(1024)(128)(2,1)} %param.8) | data formatting | bytes 14336 | tf_op jit(solution)/shard_map/reshape | solution.py:554
  1.3 0.0 copy-done
  1.3 0.7 copy.8.ids_ref
  2.1 2.3 %copy.9.router_ref = bf16[3584,64]{1,0:T(8,128)(2,1)} copy(bf16[3584,64]{0,1:T(8,128)(2,1)} %param.9) | data formatting | bytes 917504 | tf_op args[2]
  4.3 105.5 %shard_map.73 = bf16[128,448]{1,0:T(8,128)(2,1)} custom-call(s32[128,3]{1,0:T(8,128)} %copy.8.ids_ref, bf16[128,3584]{1,0:T(8,128)(2,1)} %tok_ref.1, bf16[1,3584]{1,0:T(2,128)(2,1)} %reshape.3.gain_ref, bf16[3584,64]{1,0:T(8,128)(2,1)} %copy.9.router_ref, bf16[1,3584,128]{2,1,0:T(8,128)(2,1)} %wg_hbm.1, bf16[1,3584,128]{2,1,0:T(8,128)(2,1)} %wu_hbm.1, ...), custom_call_target="tpu_custom_call" | custom-call | tf_op jit(solution)/shard_map/pallas_call | solution.py:515
  109.9 1.7 %copy.10 = bf16[128,448]{0,1:T(8,128)(2,1)} copy(bf16[128,448]{1,0:T(8,128)(2,1)} %shard_map.73) | data formatting | bytes 229376 | tf_op jit(solution)/shard_map/pallas_call | solution.py:515
Async XLA Ops:
  0.0 1.3 %copy-start = (s32[128,3]{0,1:T(4,128)S(1)}, s32[128,3]{0,1:T(4,128)}, u32[]{:S(2)}) copy-start(s32[128,3]{0,1:T(4,128)} %param.13) | copy-start | bytes 4612
